TPU v7x, 32 devices: a whole 2x2x4 slice. The times are simulated.
32 devices in a mesh: row: 4 (over y, x), col: 8 (over z, core).
Axes of the slice: x: 2, y: 2, z: 4, core: 2. Of those that a mesh axis runs over, the one named last changes fastest.
Arguments:
- pair_repr: bfloat16 [1024, 1024, 128], P('row', 'col'), may hold values from -6 to 6
- logit_cotangent: bfloat16 [1024, 1024, 128], P('row', 'col'), may hold values from -6 to 6
- pair_mask: int32 [1024, 1024], P('row', 'col'), may hold values 0 or 1
- single_repr: bfloat16 [1024, 384], P(('row', 'col')), may hold values from -6 to 6
- token_index: int32 [1024], replicated, may hold values from 0 to 2046, as said below
- pair_up: bfloat16 [128, 512], replicated, may hold values from -0.5 to 0.5
- pair_gate: bfloat16 [128, 512], replicated, may hold values from -0.5 to 0.5
- pair_down: bfloat16 [512, 128], replicated, may hold values from -0.25 to 0.25
- head_weight: bfloat16 [128, 128], replicated, may hold values from -0.5 to 0.5
- rel_table: bfloat16 [65, 128], replicated, may hold values from -3 to 3
- proj_row: bfloat16 [384, 128], replicated, may hold values from -0.3125 to 0.3125
- proj_col: bfloat16 [384, 128], replicated, may hold values from -0.3125 to 0.3125
- single_gate: bfloat16 [384, 1536], replicated, may hold values from -0.3125 to 0.3125
- single_up: bfloat16 [384, 1536], replicated, may hold values from -0.3125 to 0.3125
- single_down: bfloat16 [1536, 384], replicated, may hold values from -0.15625 to 0.15625
Outputs:
- pair_grad: bfloat16 [1024, 1024, 128], P('row', 'col')
- single_grad: bfloat16 [1024, 384], P(('row', 'col'))
- grad_pair_up: float32 [128, 512], replicated
- grad_pair_gate: float32 [128, 512], replicated
- grad_pair_down: float32 [512, 128], replicated
- grad_head: float32 [128, 128], replicated
- grad_rel: float32 [65, 128], replicated
- grad_proj_row: float32 [384, 128], replicated
- grad_proj_col: float32 [384, 128], replicated
- grad_single_gate: float32 [384, 1536], P(None, ('row', 'col'))
- grad_single_up: float32 [384, 1536], P(None, ('row', 'col'))
- grad_single_down: float32 [1536, 384], P(('row', 'col'))
Inputs may be any that keep to these rules, and one draw needn't show every extreme that they name: `token_index`: strictly increasing, entry 0 is 0, successive entries differ by 1 to 3, the last entry is 2046.
All inputs are finite; a program needn't handle non-finite values. No bound on the sum of `pair_mask` on one device may be relied on, other than what follows from the above.
Results may differ from a plain program's by a relative error of at most 0.018.
Values may be sent and summed in bfloat16 or wider, within the bound.
No kernel may reach another device: no remote copies, remote signals or barrier semaphores. Data moves between devices by JAX's collectives and lax.ppermute only.
A program may use at most 192 MiB of HBM per device.

v0:
```python
import jax
import jax.numpy as jnp
from jax import lax
from jax.sharding import PartitionSpec as P

norm_eps = 1e-05


def gated_parts(gate):
    sigma = jax.nn.sigmoid(gate)
    return (gate * sigma, sigma * (1.0 + gate * (1.0 - sigma)))


def product(matrix_a, matrix_b):
    return jnp.dot(matrix_a, matrix_b, preferred_element_type=jnp.float32)


def product_left(matrix_a, matrix_b):
    return lax.dot_general(
        matrix_a, matrix_b, (((0,), (0,)), ((), ())), preferred_element_type=jnp.float32
    )


def product_right(matrix_a, matrix_b):
    return lax.dot_general(
        matrix_a, matrix_b, (((1,), (1,)), ((), ())), preferred_element_type=jnp.float32
    )


def single_forward(single_repr, single_gate, single_up, single_down):
    source = single_repr.astype(jnp.float32)
    inverse_rms = lax.rsqrt(jnp.mean(source * source, axis=-1, keepdims=True) + norm_eps)
    normed = source * inverse_rms
    normed_bf = normed.astype(jnp.bfloat16)
    gate_pre = product(normed_bf, single_gate)
    up_pre = product(normed_bf, single_up)
    silu_value, silu_slope = gated_parts(gate_pre)
    hidden = (silu_value * up_pre).astype(jnp.bfloat16)
    updated = (source + product(hidden, single_down)).astype(jnp.bfloat16)
    return (normed, inverse_rms, normed_bf, up_pre, silu_value, silu_slope, hidden, updated)


def single_backward(grad_in, saved_state, single_gate, single_up, single_down):
    normed, inverse_rms, normed_bf, up_pre, silu_value, silu_slope, hidden, updated = saved_state
    grad_bf = grad_in.astype(jnp.bfloat16)
    grad_hidden = product_right(grad_bf, single_down)
    grad_up = (grad_hidden * silu_value).astype(jnp.bfloat16)
    grad_gate = (grad_hidden * up_pre * silu_slope).astype(jnp.bfloat16)
    grad_normed = product_right(grad_gate, single_gate) + product_right(grad_up, single_up)
    grad_source = grad_in + inverse_rms * (
        grad_normed - normed * jnp.mean(grad_normed * normed, axis=-1, keepdims=True)
    )
    return (grad_source, grad_bf, grad_gate, grad_up)


def local_weight_sums(normed_bf, grad_bf, grad_gate, grad_up, hidden):
    return jnp.stack(
        [
            product_left(normed_bf, grad_gate),
            product_left(normed_bf, grad_up),
            product_left(grad_bf, hidden),
        ],
        axis=0,
    )


def pair_block(
    pair_blk,
    cot_blk,
    mirror_blk,
    row_blk,
    col_blk,
    row_pos,
    col_pos,
    rel_table,
    up_gate,
    pair_down,
    head_weight,
):
    n_rows, n_cols, pair_width = pair_blk.shape
    bin_count = mirror_blk.shape[2]
    rel_count = rel_table.shape[0]
    rel_span = (rel_count - 1) // 2
    pair_count = n_rows * n_cols
    offset = jnp.clip(row_pos[:, None] - col_pos[None, :], -rel_span, rel_span) + rel_span
    one_hot = offset.reshape(pair_count, 1) == jnp.arange(rel_count, dtype=jnp.int32)[None, :]
    hot_table = one_hot.astype(jnp.bfloat16)
    pair_in = (
        pair_blk.astype(jnp.float32)
        + row_blk.astype(jnp.float32)[:, None, :]
        + col_blk.astype(jnp.float32)[None, :, :]
    )
    pair_in = pair_in.reshape(pair_count, pair_width) + product(hot_table, rel_table)
    centred = pair_in - jnp.mean(pair_in, axis=-1, keepdims=True)
    inv_std = lax.rsqrt(jnp.mean(centred * centred, axis=-1, keepdims=True) + norm_eps)
    normed = centred * inv_std
    normed_bf = normed.astype(jnp.bfloat16)
    hidden_width = up_gate.shape[1] // 2
    both_pre = product(normed_bf, up_gate)
    up_pre = both_pre[:, :hidden_width]
    gate_pre = both_pre[:, hidden_width:]
    silu_value, silu_slope = gated_parts(gate_pre)
    hidden = (silu_value * up_pre).astype(jnp.bfloat16)
    pair_out = (pair_in + product(hidden, pair_down)).astype(jnp.bfloat16)
    cot_flat = cot_blk.reshape(pair_count, 2 * bin_count)
    symmetric = (
        cot_flat[:, bin_count:].astype(jnp.float32)
        + mirror_blk.reshape(pair_count, bin_count).astype(jnp.float32)
    ).astype(jnp.bfloat16)
    head_cot = jnp.concatenate([cot_flat[:, :bin_count], symmetric], axis=1)
    grad_out = product_right(head_cot, head_weight)
    grad_out_bf = grad_out.astype(jnp.bfloat16)
    grad_hidden = product_right(grad_out_bf, pair_down)
    grad_both = jnp.concatenate(
        [
            (grad_hidden * silu_value).astype(jnp.bfloat16),
            (grad_hidden * up_pre * silu_slope).astype(jnp.bfloat16),
        ],
        axis=1,
    )
    grad_normed = product_right(grad_both, up_gate)
    grad_in = grad_out + inv_std * (
        grad_normed
        - jnp.mean(grad_normed, axis=-1, keepdims=True)
        - normed * jnp.mean(grad_normed * normed, axis=-1, keepdims=True)
    )
    head_sum = product_left(pair_out, head_cot)
    down_sum = product_left(hidden, grad_out_bf)
    up_gate_sum = product_left(normed_bf, grad_both)
    rel_sum = lax.dot_general(
        one_hot.astype(jnp.float32),
        grad_in,
        (((0,), (0,)), ((), ())),
        precision=lax.Precision.HIGHEST,
        preferred_element_type=jnp.float32,
    )
    grad_tile = grad_in.reshape(n_rows, n_cols, pair_width)
    return (
        grad_tile.astype(jnp.bfloat16),
        jnp.sum(grad_tile, axis=1),
        jnp.sum(grad_tile, axis=0),
        up_gate_sum,
        down_sum,
        head_sum,
        rel_sum,
    )


def local(
    pair_repr,
    logit_cotangent,
    pair_mask,
    single_repr,
    token_index,
    pair_up,
    pair_gate,
    pair_down,
    head_weight,
    rel_table,
    proj_row,
    proj_col,
    single_gate,
    single_up,
    single_down,
):
    n_row = lax.axis_size("row")
    n_col = lax.axis_size("col")
    row_index = lax.axis_index("row")
    col_index = lax.axis_index("col")
    joint_index = row_index * n_col + col_index
    tile_rows, tile_cols, pair_width = pair_repr.shape
    bin_count = logit_cotangent.shape[2] // 2
    strip_len = single_repr.shape[0]
    tokens_all = strip_len * n_row * n_col
    hidden_width = pair_up.shape[1]
    saved_state = single_forward(single_repr, single_gate, single_up, single_down)
    updated = saved_state[7]
    row_piece = product(updated, proj_row).astype(jnp.bfloat16)
    col_piece = product(updated, proj_col).astype(jnp.bfloat16)
    row_proj = lax.all_gather(row_piece, "col", axis=0, tiled=True)
    col_whole = lax.all_gather(col_piece, ("row", "col"), axis=0, tiled=True)
    col_proj = lax.dynamic_slice_in_dim(col_whole, col_index * tile_cols, tile_cols, 0)
    masked = logit_cotangent * pair_mask[:, :, None].astype(jnp.bfloat16)
    distance_part = masked[:, :, bin_count:].reshape(tile_rows, tile_cols * bin_count)
    strips = lax.all_to_all(distance_part, "col", split_axis=0, concat_axis=1, tiled=True)
    columns = lax.all_to_all(strips, ("row", "col"), split_axis=1, concat_axis=0, tiled=True)
    returned = lax.all_to_all(columns, "col", split_axis=0, concat_axis=1, tiled=True)
    mirrored = returned.reshape(tile_cols, tile_rows, bin_count).transpose(1, 0, 2)
    up_gate = jnp.concatenate([pair_up, pair_gate], axis=1)
    row_pos = lax.dynamic_slice_in_dim(token_index, row_index * tile_rows, tile_rows, 0)
    col_pos = lax.dynamic_slice_in_dim(token_index, col_index * tile_cols, tile_cols, 0)
    block_count = 4
    block_rows = tile_rows // block_count

    def block_step(running, inputs):
        pair_blk, cot_blk, mirror_blk, row_blk, pos_blk = inputs
        grad_blk, row_sum, col_sum, up_gate_sum, down_sum, head_sum, rel_sum = pair_block(
            pair_blk,
            cot_blk,
            mirror_blk,
            row_blk,
            col_proj,
            pos_blk,
            col_pos,
            rel_table,
            up_gate,
            pair_down,
            head_weight,
        )
        running = (
            running[0] + col_sum,
            running[1] + up_gate_sum,
            running[2] + down_sum,
            running[3] + head_sum,
            running[4] + rel_sum,
        )
        return (running, (grad_blk, row_sum))

    initial = (
        jnp.zeros((tile_cols, pair_width), jnp.float32),
        jnp.zeros(up_gate.shape, jnp.float32),
        jnp.zeros(pair_down.shape, jnp.float32),
        jnp.zeros(head_weight.shape, jnp.float32),
        jnp.zeros(rel_table.shape, jnp.float32),
    )
    sliced = (
        pair_repr.reshape(block_count, block_rows, tile_cols, pair_width),
        masked.reshape(block_count, block_rows, tile_cols, 2 * bin_count),
        mirrored.reshape(block_count, block_rows, tile_cols, bin_count),
        row_proj.reshape(block_count, block_rows, pair_width),
        row_pos.reshape(block_count, block_rows),
    )
    sums_out, blocks_out = lax.scan(block_step, initial, sliced)
    col_total, up_gate_sum, down_sum, head_sum, rel_sum = sums_out
    grad_blocks, row_sums = blocks_out
    pair_grad = grad_blocks.reshape(tile_rows, tile_cols, pair_width)
    row_tile = row_sums.reshape(tile_rows, pair_width)
    row_part = lax.psum_scatter(
        row_tile.astype(jnp.bfloat16), "col", scatter_dimension=0, tiled=True
    )
    col_summed = lax.psum(col_total.astype(jnp.bfloat16), "row")
    col_every = lax.all_gather(col_summed, "col", axis=0, tiled=True)
    col_bf = lax.dynamic_slice_in_dim(col_every, joint_index * strip_len, strip_len, 0)
    single_cot = product_right(row_part, proj_row) + product_right(col_bf, proj_col)
    prow_sum = product_left(updated, row_part)
    pcol_sum = product_left(updated, col_bf)
    grad_source, grad_bf, grad_gate, grad_up = single_backward(
        single_cot, saved_state, single_gate, single_up, single_down
    )
    normed_bf = saved_state[2]
    hidden = saved_state[6]
    stacked = local_weight_sums(normed_bf, grad_bf, grad_gate, grad_up, hidden)
    summed = lax.psum(stacked, ("row", "col"))
    share_len = summed.shape[2] // (n_row * n_col)
    own_share = lax.dynamic_slice_in_dim(summed, joint_index * share_len, share_len, 2)
    totals = lax.psum(
        (up_gate_sum, down_sum, head_sum, rel_sum, prow_sum, pcol_sum), ("row", "col")
    )
    grad_scale = 1.0 / tokens_all
    return (
        pair_grad,
        grad_source.astype(jnp.bfloat16),
        totals[0][:, :hidden_width] * grad_scale,
        totals[0][:, hidden_width:] * grad_scale,
        totals[1] * grad_scale,
        totals[2] * grad_scale,
        totals[3] * grad_scale,
        totals[4] * grad_scale,
        totals[5] * grad_scale,
        own_share[0] * grad_scale,
        own_share[1] * grad_scale,
        jnp.transpose(own_share[2]) * grad_scale,
    )


def solution(mesh):
    placed = (
        P("row", "col", None),
        P("row", "col", None),
        P("row", "col"),
        P(("row", "col"), None),
        P(),
        P(),
        P(),
        P(),
        P(),
        P(),
        P(),
        P(),
        P(),
        P(),
        P(),
    )
    return jax.shard_map(
        local,
        mesh=mesh,
        in_specs=placed,
        out_specs=(
            P("row", "col", None),
            P(("row", "col"), None),
            P(),
            P(),
            P(),
            P(),
            P(),
            P(),
            P(),
            P(None, ("row", "col")),
            P(None, ("row", "col")),
            P(("row", "col"), None),
        ),
        check_vma=False,
    )
```

profile of v0, /device:TPU:0, one launch (start us, length us, event | category | flops | bytes accessed | tf_op | source)
XLA Modules:
  0.0 1154.7 jit_solution(11379093476381169805)
XLA Ops:
  8.2 8.6 broadcast_multiply_fusion.3
  16.8 9.9 slice.44
  26.8 12.1 %all_to_all.36 = bf16[8,32,8192]{2,1,0:T(8,128)(2,1)} reshape(bf16[256,128,64]{2,1,0:T(8,128)(2,1)} %slice.44) | data formatting | bytes 8388608 | tf_op jit(solution)/shard_map/all_to_all | solution.py:185
  38.8 100.3 %all_to_all.48 = bf16[8,32,8192]{2,1,0:T(8,128)(2,1)S(1)} all-to-all(bf16[8,32,8192]{2,1,0:T(8,128)(2,1)} %all_to_all.36), channel_id=1, replica_groups=mesh['row'=4,'col'=8] {'col'}, dimensions={0} | all-to-all | bytes 8388608 | tf_op jit(solution)/shard_map/all_to_all | solution.py:185
  139.1 4.3 copy.44
  143.4 7.9 all_to_all.39
  151.4 4.5 copy.45
  155.8 98.3 %all_to_all.49 = bf16[32,32,2048]{2,0,1:T(8,128)(2,1)} all-to-all(bf16[32,32,2048]{2,0,1:T(8,128)(2,1)S(1)} %copy.45), channel_id=1, replica_groups=mesh['row'=4,'col'=8] {'row','col'}, dimensions={1} | all-to-all | bytes 8388608 | tf_op jit(solution)/shard_map/all_to_all | solution.py:186
  254.2 4.7 all-to-all-start.2
  265.2 94.8 %all_gather.9 = bf16[256,128]{1,0:T(8,128)(2,1)} all-gather(bf16[32,128]{1,0:T(8,128)(2,1)S(1)} %convolution_convert_fusion.1), channel_id=1, replica_groups=mesh['row'=4,'col'=8] {'col'}, dimensions={0}, use_global_device_ids=true | all-gather | bytes 73728 | tf_op jit(solution)/shard_map/all_gather | solution.py:180
  360.1 40.0 %all_gather.10 = bf16[1024,128]{1,0:T(8,128)(2,1)S(1)} all-gather(bf16[32,128]{1,0:T(8,128)(2,1)S(1)} %convolution_convert_fusion), channel_id=1, replica_groups=mesh['row'=4,'col'=8] {'row','col'}, dimensions={0}, use_global_device_ids=true | all-gather | bytes 270336 | tf_op jit(solution)/shard_map/all_gather | solution.py:181
  400.9 6.5 copy.46
  407.4 482.4 %while.23 = (s32[]{:T(128)}, f32[128,128]{1,0:T(8,128)}, f32[128,1024]{1,0:T(8,128)}, f32[512,128]{1,0:T(8,128)}, f32[128,128]{1,0:T(8,128)}, /*index=5*/f32[65,...) while((s32[]{:T(128)}, f32[128,128]{1,0:T(8,128)}, ...), condition=%wide.region_8.9_spmd.clone, body=%wide.region_1.8_spmd.clone.sunk | while | flops 11331420160 | bytes 375022848 | solution.py:233
  433.8 12.2 %fusion.127 = f32[8192,1024]{0,1:T(8,128)} fusion(bf16[128,1024]{1,0:T(8,128)(2,1)S(1)} %copy-done.9, f32[8192,128]{1,0:T(8,128)S(1)} %get-tuple-element.485, f32[8192]{0:T(1024)S(1)} %add_rsqrt_fusion.3, f32[8192]{0:T(1024)S(1)} %broadcast_multiply_fusion.13), kind=kOutput, calls=%fused_computation.53.clone.1 | convolution fusion | flops 2150629376 | bytes 38076416 | tf_op jit(solution)/shard_map/while/body/eval_jaxpr/dot_general | solution.py:15
  456.7 22.8 %multiply_convert_fusion.7 = (bf16[8192,512]{0,1:T(8,128)(2,1)}, bf16[8192,512]{0,1:T(8,128)(2,1)}, bf16[8192,512]{0,1:T(8,128)(2,1)}) fusion(f32[8192,1024]{0,1:T(8,128)} %fusion.127, bf16[512,128]{1,0:T(8,128)(2,1)S(1)} %get-tuple-element.556, f32[8192,128]{1,0:T(8,128)} %fusion.124), kind=kOutput, calls=%fused_computation.3.clone.1 | convolution fusion | flops 1137704960 | bytes 63045632 | tf_op jit(solution)/shard_map/while/body/eval_jaxpr/dot_general | solution.py:25
  479.4 13.2 %fusion.128 = (f32[8192]{0:T(1024)S(1)}, f32[8192]{0:T(1024)S(1)}, f32[8192,128]{1,0:T(8,128)S(1)}) fusion(f32[8192]{0:T(1024)S(1)} %add_rsqrt_fusion.3, f32[8192,128]{1,0:T(8,128)S(1)} %copy-done.2, f32[8192]{0:T(1024)S(1)} %broadcast_multiply_fusion.13, bf16[128,1024]{1,0:T(8,128)(2,1)S(1)} %copy-done.10, ...), kind=kOutput, calls=%fused_computation.108.clone.1 | convolution fusion | flops 2186264576 | bytes 25559040 | tf_op jit(solution)/shard_map/while/body/eval_jaxpr/dot_general | solution.py:25
  492.7 5.0 bitcast_reduce_fusion.2
  500.8 11.2 fusion.130
  512.1 7.8 convolution_add_fusion.7
  519.9 12.5 %fusion.129 = f32[128,1024]{1,0:T(8,128)S(1)} fusion(bf16[8192,512]{0,1:T(8,128)(2,1)} %get-tuple-element.487, bf16[8192,512]{0,1:T(8,128)(2,1)} %get-tuple-element.488, f32[128,1024]{1,0:T(8,128)S(1)} %copy-done.26, pred[]{:T(512)S(6)} %compare.3, f32[8192,128]{1,0:T(8,128)S(1)} %copy-done.3, f32[8192]{0:T(1024)S(1)} %add_rsqrt_fusion.3, ...), kind=kOutput, calls=%fused_computation.23.clone.1 | convolution fusion | flops 2184445952 | bytes 22085632 | tf_op jit(solution)/shard_map/while/body/eval_jaxpr/dot_general | solution.py:19
  535.1 4.2 fusion.131
  550.4 12.2 %fusion.127 = f32[8192,1024]{0,1:T(8,128)} fusion(bf16[128,1024]{1,0:T(8,128)(2,1)S(1)} %copy-done.9, f32[8192,128]{1,0:T(8,128)S(1)} %get-tuple-element.485, f32[8192]{0:T(1024)S(1)} %add_rsqrt_fusion.3, f32[8192]{0:T(1024)S(1)} %broadcast_multiply_fusion.13), kind=kOutput, calls=%fused_computation.53.clone.1 | convolution fusion | flops 2150629376 | bytes 38076416 | tf_op jit(solution)/shard_map/while/body/eval_jaxpr/dot_general | solution.py:15
  573.2 22.8 %multiply_convert_fusion.7 = (bf16[8192,512]{0,1:T(8,128)(2,1)}, bf16[8192,512]{0,1:T(8,128)(2,1)}, bf16[8192,512]{0,1:T(8,128)(2,1)}) fusion(f32[8192,1024]{0,1:T(8,128)} %fusion.127, bf16[512,128]{1,0:T(8,128)(2,1)S(1)} %get-tuple-element.556, f32[8192,128]{1,0:T(8,128)} %fusion.124), kind=kOutput, calls=%fused_computation.3.clone.1 | convolution fusion | flops 1137704960 | bytes 63045632 | tf_op jit(solution)/shard_map/while/body/eval_jaxpr/dot_general | solution.py:25
  596.0 13.2 %fusion.128 = (f32[8192]{0:T(1024)S(1)}, f32[8192]{0:T(1024)S(1)}, f32[8192,128]{1,0:T(8,128)S(1)}) fusion(f32[8192]{0:T(1024)S(1)} %add_rsqrt_fusion.3, f32[8192,128]{1,0:T(8,128)S(1)} %copy-done.2, f32[8192]{0:T(1024)S(1)} %broadcast_multiply_fusion.13, bf16[128,1024]{1,0:T(8,128)(2,1)S(1)} %copy-done.10, ...), kind=kOutput, calls=%fused_computation.108.clone.1 | convolution fusion | flops 2186264576 | bytes 25559040 | tf_op jit(solution)/shard_map/while/body/eval_jaxpr/dot_general | solution.py:25
  609.3 5.0 bitcast_reduce_fusion.2
  617.4 11.2 fusion.130
  628.6 7.8 convolution_add_fusion.7
  636.4 12.5 %fusion.129 = f32[128,1024]{1,0:T(8,128)S(1)} fusion(bf16[8192,512]{0,1:T(8,128)(2,1)} %get-tuple-element.487, bf16[8192,512]{0,1:T(8,128)(2,1)} %get-tuple-element.488, f32[128,1024]{1,0:T(8,128)S(1)} %copy-done.26, pred[]{:T(512)S(6)} %compare.3, f32[8192,128]{1,0:T(8,128)S(1)} %copy-done.3, f32[8192]{0:T(1024)S(1)} %add_rsqrt_fusion.3, ...), kind=kOutput, calls=%fused_computation.23.clone.1 | convolution fusion | flops 2184445952 | bytes 22085632 | tf_op jit(solution)/shard_map/while/body/eval_jaxpr/dot_general | solution.py:19
  666.9 12.2 %fusion.127 = f32[8192,1024]{0,1:T(8,128)} fusion(bf16[128,1024]{1,0:T(8,128)(2,1)S(1)} %copy-done.9, f32[8192,128]{1,0:T(8,128)S(1)} %get-tuple-element.485, f32[8192]{0:T(1024)S(1)} %add_rsqrt_fusion.3, f32[8192]{0:T(1024)S(1)} %broadcast_multiply_fusion.13), kind=kOutput, calls=%fused_computation.53.clone.1 | convolution fusion | flops 2150629376 | bytes 38076416 | tf_op jit(solution)/shard_map/while/body/eval_jaxpr/dot_general | solution.py:15
  689.8 22.8 %multiply_convert_fusion.7 = (bf16[8192,512]{0,1:T(8,128)(2,1)}, bf16[8192,512]{0,1:T(8,128)(2,1)}, bf16[8192,512]{0,1:T(8,128)(2,1)}) fusion(f32[8192,1024]{0,1:T(8,128)} %fusion.127, bf16[512,128]{1,0:T(8,128)(2,1)S(1)} %get-tuple-element.556, f32[8192,128]{1,0:T(8,128)} %fusion.124), kind=kOutput, calls=%fused_computation.3.clone.1 | convolution fusion | flops 1137704960 | bytes 63045632 | tf_op jit(solution)/shard_map/while/body/eval_jaxpr/dot_general | solution.py:25
  712.5 13.2 %fusion.128 = (f32[8192]{0:T(1024)S(1)}, f32[8192]{0:T(1024)S(1)}, f32[8192,128]{1,0:T(8,128)S(1)}) fusion(f32[8192]{0:T(1024)S(1)} %add_rsqrt_fusion.3, f32[8192,128]{1,0:T(8,128)S(1)} %copy-done.2, f32[8192]{0:T(1024)S(1)} %broadcast_multiply_fusion.13, bf16[128,1024]{1,0:T(8,128)(2,1)S(1)} %copy-done.10, ...), kind=kOutput, calls=%fused_computation.108.clone.1 | convolution fusion | flops 2186264576 | bytes 25559040 | tf_op jit(solution)/shard_map/while/body/eval_jaxpr/dot_general | solution.py:25
  725.8 5.0 bitcast_reduce_fusion.2
  733.9 11.2 fusion.130
  745.2 7.8 convolution_add_fusion.7
  753.0 12.5 %fusion.129 = f32[128,1024]{1,0:T(8,128)S(1)} fusion(bf16[8192,512]{0,1:T(8,128)(2,1)} %get-tuple-element.487, bf16[8192,512]{0,1:T(8,128)(2,1)} %get-tuple-element.488, f32[128,1024]{1,0:T(8,128)S(1)} %copy-done.26, pred[]{:T(512)S(6)} %compare.3, f32[8192,128]{1,0:T(8,128)S(1)} %copy-done.3, f32[8192]{0:T(1024)S(1)} %add_rsqrt_fusion.3, ...), kind=kOutput, calls=%fused_computation.23.clone.1 | convolution fusion | flops 2184445952 | bytes 22085632 | tf_op jit(solution)/shard_map/while/body/eval_jaxpr/dot_general | solution.py:19
  768.2 4.2 fusion.131
  783.5 12.2 %fusion.127 = f32[8192,1024]{0,1:T(8,128)} fusion(bf16[128,1024]{1,0:T(8,128)(2,1)S(1)} %copy-done.9, f32[8192,128]{1,0:T(8,128)S(1)} %get-tuple-element.485, f32[8192]{0:T(1024)S(1)} %add_rsqrt_fusion.3, f32[8192]{0:T(1024)S(1)} %broadcast_multiply_fusion.13), kind=kOutput, calls=%fused_computation.53.clone.1 | convolution fusion | flops 2150629376 | bytes 38076416 | tf_op jit(solution)/shard_map/while/body/eval_jaxpr/dot_general | solution.py:15
  806.3 22.8 %multiply_convert_fusion.7 = (bf16[8192,512]{0,1:T(8,128)(2,1)}, bf16[8192,512]{0,1:T(8,128)(2,1)}, bf16[8192,512]{0,1:T(8,128)(2,1)}) fusion(f32[8192,1024]{0,1:T(8,128)} %fusion.127, bf16[512,128]{1,0:T(8,128)(2,1)S(1)} %get-tuple-element.556, f32[8192,128]{1,0:T(8,128)} %fusion.124), kind=kOutput, calls=%fused_computation.3.clone.1 | convolution fusion | flops 1137704960 | bytes 63045632 | tf_op jit(solution)/shard_map/while/body/eval_jaxpr/dot_general | solution.py:25
  829.1 13.2 %fusion.128 = (f32[8192]{0:T(1024)S(1)}, f32[8192]{0:T(1024)S(1)}, f32[8192,128]{1,0:T(8,128)S(1)}) fusion(f32[8192]{0:T(1024)S(1)} %add_rsqrt_fusion.3, f32[8192,128]{1,0:T(8,128)S(1)} %copy-done.2, f32[8192]{0:T(1024)S(1)} %broadcast_multiply_fusion.13, bf16[128,1024]{1,0:T(8,128)(2,1)S(1)} %copy-done.10, ...), kind=kOutput, calls=%fused_computation.108.clone.1 | convolution fusion | flops 2186264576 | bytes 25559040 | tf_op jit(solution)/shard_map/while/body/eval_jaxpr/dot_general | solution.py:25
  842.3 5.0 bitcast_reduce_fusion.2
  850.5 11.2 fusion.130
  861.7 7.8 convolution_add_fusion.7
  869.5 12.5 %fusion.129 = f32[128,1024]{1,0:T(8,128)S(1)} fusion(bf16[8192,512]{0,1:T(8,128)(2,1)} %get-tuple-element.487, bf16[8192,512]{0,1:T(8,128)(2,1)} %get-tuple-element.488, f32[128,1024]{1,0:T(8,128)S(1)} %copy-done.26, pred[]{:T(512)S(6)} %compare.3, f32[8192,128]{1,0:T(8,128)S(1)} %copy-done.3, f32[8192]{0:T(1024)S(1)} %add_rsqrt_fusion.3, ...), kind=kOutput, calls=%fused_computation.23.clone.1 | convolution fusion | flops 2184445952 | bytes 22085632 | tf_op jit(solution)/shard_map/while/body/eval_jaxpr/dot_general | solution.py:19
  890.7 14.0 %psum.56 = bf16[128,128]{1,0:T(8,128)(2,1)S(1)} all-reduce(bf16[128,128]{1,0:T(8,128)(2,1)S(1)} %convert_element_type.121), channel_id=1, replica_groups=mesh['row'=4,'col'=8] {'row'}, use_global_device_ids=true, to_apply=%region_10.11 | all-reduce | flops 16384 | bytes 65536 | tf_op jit(solution)/shard_map/psum | solution.py:241
  904.6 14.2 %all_gather.11 = bf16[1024,128]{1,0:T(8,128)(2,1)S(1)} all-gather(bf16[128,128]{1,0:T(8,128)(2,1)S(1)} %psum.56), channel_id=1, replica_groups=mesh['row'=4,'col'=8] {'col'}, dimensions={0}, use_global_device_ids=true | all-gather | bytes 294912 | tf_op jit(solution)/shard_map/all_gather | solution.py:242
  920.5 26.6 %reduce-scatter.2.cloned.1.call-done = bf16[32,128]{1,0:T(8,128)(2,1)} async-done(((bf16[256,128]{1,0:T(8,128)(2,1)}), bf16[32,128]{1,0:T(8,128)(2,1)}) %reduce-scatter.2.cloned.1.call-update) | async-done | bytes 8208 | tf_op jit(solution)/shard_map/reduce_scatter | solution.py:238
  958.8 40.0 %psum.60 = f32[65,128]{1,0:T(8,128)S(1)} all-reduce(f32[65,128]{1,0:T(8,128)S(1)} %copy-done.20), channel_id=1, replica_groups=mesh['row'=4,'col'=8] {'row','col'}, use_global_device_ids=true, to_apply=%region_15.16 | all-reduce | flops 8320 | bytes 66560 | tf_op jit(solution)/shard_map/psum | solution.py:256
  1001.2 135.8 %all-reduce.3.cloned.1.call-done = (f32[128,1024]{1,0:T(8,128)}, f32[512,128]{1,0:T(8,128)}, f32[128,128]{1,0:T(8,128)}, f32[384,128]{1,0:T(8,128)}, f32[384,128]{1,0:T(8,128)}, /*index=5*/f32[3,384,1536]{2,1,0:T(8,128)}) async-done(((f32[128,1024]{1,0:T(8,128)}, f32[512,128]{1,0:T(8,128)}, f32[128,128]{1,0:T(8,128)}, f32[384,128]{1,0:T(8,128)}, f32[384,128]{1,0:T(8,128)}, ...) | async-done | bytes 8323088 | tf_op jit(solution)/shard_map/psum | solution.py:256
  (314 shorter events, 152.7 us)
Async XLA Ops:
  7.2 255.2 %copy-start = (bf16[384,1536]{1,0:T(8,128)(2,1)S(1)}, bf16[384,1536]{1,0:T(8,128)(2,1)}, u32[]{:S(2)}) copy-start(bf16[384,1536]{1,0:T(8,128)(2,1)} %param.30) | copy-start | bytes 3538948
  254.2 7.7 copy-start.16
  254.2 7.8 copy-start.11
  254.2 146.7 %all-to-all-start.2 = ((bf16[8,128,2048]{2,1,0:T(8,128)(2,1)}), bf16[8,128,2048]{2,1,0:T(8,128)(2,1)}, u32[]{:S(2)}, u32[]{:S(2)}) async-start(bf16[8,128,2048]{2,1,0:T(8,128)(2,1)} %bitcast.135), calls=%async_computation.2 | async-start | bytes 8388608 | tf_op jit(solution)/shard_map/all_to_all | solution.py:187
  258.9 101.1 %copy-start.30 = (bf16[384,128]{1,0:T(8,128)(2,1)S(1)}, bf16[384,128]{1,0:T(8,128)(2,1)}, u32[]{:S(2)}) copy-start(bf16[384,128]{1,0:T(8,128)(2,1)} %param.28) | copy-start | bytes 294916
  258.9 141.3 %copy-start.31 = (bf16[128,512]{1,0:T(8,128)(2,1)S(1)}, bf16[128,512]{1,0:T(8,128)(2,1)}, u32[]{:S(2)}) copy-start(bf16[128,512]{1,0:T(8,128)(2,1)} %param.23) | copy-start | bytes 393220
  258.9 141.3 %copy-start.32 = (bf16[128,512]{1,0:T(8,128)(2,1)S(1)}, bf16[128,512]{1,0:T(8,128)(2,1)}, u32[]{:S(2)}) copy-start(bf16[128,512]{1,0:T(8,128)(2,1)} %param.22) | copy-start | bytes 393220
  258.9 688.2 %reduce-scatter.2.cloned.1.call-start = ((), (), s32[]{:S(2)}) async-start(), calls=%async_computation.4 | async-start | bytes 73728 | tf_op jit(solution)/shard_map/reduce_scatter | solution.py:238
  262.3 137.8 %copy-start.23 = (f32[32,1536]{1,0:T(8,128)}, f32[32,1536]{1,0:T(8,128)S(1)}, u32[]{:S(2)}) copy-start(f32[32,1536]{1,0:T(8,128)S(1)} %fusion.52) | copy-start | bytes 589828
  263.4 96.7 %copy-start.21 = (bf16[32,1536]{1,0:T(8,128)(2,1)}, bf16[32,1536]{1,0:T(8,128)(2,1)S(1)}, u32[]{:S(2)}) copy-start(bf16[32,1536]{1,0:T(8,128)(2,1)S(1)} %get-tuple-element.350) | copy-start | bytes 294916
  265.0 135.1 %copy-start.24 = (bf16[32,384]{1,0:T(8,128)(2,1)}, bf16[32,384]{1,0:T(8,128)(2,1)S(1)}, u32[]{:S(2)}) copy-start(bf16[32,384]{1,0:T(8,128)(2,1)S(1)} %fusion.26) | copy-start | bytes 73732
  400.9 6.5 copy-start.13
  425.9 27.5 %copy-start.6 = (bf16[1,64,128,128]{3,2,1,0:T(8,128)(2,1)}, bf16[1,64,128,128]{3,2,1,0:T(8,128)(2,1)S(1)}, u32[]{:S(2)}) copy-start(bf16[1,64,128,128]{3,2,1,0:T(8,128)(2,1)S(1)} %get-tuple-element.483) | copy-start | bytes 6291460 | tf_op jit(solution)/shard_map/while
  431.3 14.7 %copy-start.1 = (f32[8192,128]{1,0:T(8,128)}, f32[8192,128]{1,0:T(8,128)S(1)}, u32[]{:S(2)}) copy-start(f32[8192,128]{1,0:T(8,128)S(1)} %get-tuple-element.485) | copy-start | bytes 12582916 | tf_op jit(solution)/shard_map/while
  456.7 22.8 %copy-start.2 = (f32[8192,128]{1,0:T(8,128)S(1)}, f32[8192,128]{1,0:T(8,128)}, u32[]{:S(2)}) copy-start(f32[8192,128]{1,0:T(8,128)} %copy-done.1) | copy-start | bytes 12582916 | tf_op jit(solution)/shard_map/while
  456.7 22.8 %copy-start.10 = (bf16[128,1024]{1,0:T(8,128)(2,1)S(1)}, bf16[128,1024]{1,0:T(8,128)(2,1)}, u32[]{:S(2)}) copy-start(bf16[128,1024]{1,0:T(8,128)(2,1)} %get-tuple-element.557) | copy-start | bytes 786436 | tf_op jit(solution)/shard_map/while
  479.4 13.3 %copy-start.5 = (f32[8192,128]{1,0:T(8,128)S(1)}, f32[8192,128]{1,0:T(8,128)}, u32[]{:S(2)}) copy-start(f32[8192,128]{1,0:T(8,128)} %fusion.124) | copy-start | bytes 12582916 | tf_op jit(solution)/shard_map/while
  512.1 7.8 copy-start.3
  512.1 7.8 copy-start.26
  532.4 6.9 copy-start.27
  542.5 27.5 %copy-start.6 = (bf16[1,64,128,128]{3,2,1,0:T(8,128)(2,1)}, bf16[1,64,128,128]{3,2,1,0:T(8,128)(2,1)S(1)}, u32[]{:S(2)}) copy-start(bf16[1,64,128,128]{3,2,1,0:T(8,128)(2,1)S(1)} %get-tuple-element.483) | copy-start | bytes 6291460 | tf_op jit(solution)/shard_map/while
  547.8 14.7 %copy-start.1 = (f32[8192,128]{1,0:T(8,128)}, f32[8192,128]{1,0:T(8,128)S(1)}, u32[]{:S(2)}) copy-start(f32[8192,128]{1,0:T(8,128)S(1)} %get-tuple-element.485) | copy-start | bytes 12582916 | tf_op jit(solution)/shard_map/while
  573.2 22.8 %copy-start.2 = (f32[8192,128]{1,0:T(8,128)S(1)}, f32[8192,128]{1,0:T(8,128)}, u32[]{:S(2)}) copy-start(f32[8192,128]{1,0:T(8,128)} %copy-done.1) | copy-start | bytes 12582916 | tf_op jit(solution)/shard_map/while
  573.2 22.8 %copy-start.10 = (bf16[128,1024]{1,0:T(8,128)(2,1)S(1)}, bf16[128,1024]{1,0:T(8,128)(2,1)}, u32[]{:S(2)}) copy-start(bf16[128,1024]{1,0:T(8,128)(2,1)} %get-tuple-element.557) | copy-start | bytes 786436 | tf_op jit(solution)/shard_map/while
  596.0 13.3 %copy-start.5 = (f32[8192,128]{1,0:T(8,128)S(1)}, f32[8192,128]{1,0:T(8,128)}, u32[]{:S(2)}) copy-start(f32[8192,128]{1,0:T(8,128)} %fusion.124) | copy-start | bytes 12582916 | tf_op jit(solution)/shard_map/while
  628.6 7.8 copy-start.3
  628.6 7.8 copy-start.26
  649.0 6.9 copy-start.27
  659.0 27.5 %copy-start.6 = (bf16[1,64,128,128]{3,2,1,0:T(8,128)(2,1)}, bf16[1,64,128,128]{3,2,1,0:T(8,128)(2,1)S(1)}, u32[]{:S(2)}) copy-start(bf16[1,64,128,128]{3,2,1,0:T(8,128)(2,1)S(1)} %get-tuple-element.483) | copy-start | bytes 6291460 | tf_op jit(solution)/shard_map/while
  664.4 14.7 %copy-start.1 = (f32[8192,128]{1,0:T(8,128)}, f32[8192,128]{1,0:T(8,128)S(1)}, u32[]{:S(2)}) copy-start(f32[8192,128]{1,0:T(8,128)S(1)} %get-tuple-element.485) | copy-start | bytes 12582916 | tf_op jit(solution)/shard_map/while
  689.8 22.8 %copy-start.2 = (f32[8192,128]{1,0:T(8,128)S(1)}, f32[8192,128]{1,0:T(8,128)}, u32[]{:S(2)}) copy-start(f32[8192,128]{1,0:T(8,128)} %copy-done.1) | copy-start | bytes 12582916 | tf_op jit(solution)/shard_map/while
  689.8 22.8 %copy-start.10 = (bf16[128,1024]{1,0:T(8,128)(2,1)S(1)}, bf16[128,1024]{1,0:T(8,128)(2,1)}, u32[]{:S(2)}) copy-start(bf16[128,1024]{1,0:T(8,128)(2,1)} %get-tuple-element.557) | copy-start | bytes 786436 | tf_op jit(solution)/shard_map/while
  712.5 13.3 %copy-start.5 = (f32[8192,128]{1,0:T(8,128)S(1)}, f32[8192,128]{1,0:T(8,128)}, u32[]{:S(2)}) copy-start(f32[8192,128]{1,0:T(8,128)} %fusion.124) | copy-start | bytes 12582916 | tf_op jit(solution)/shard_map/while
  745.2 7.8 copy-start.3
  745.2 7.8 copy-start.26
  765.5 6.9 copy-start.27
  775.6 27.5 %copy-start.6 = (bf16[1,64,128,128]{3,2,1,0:T(8,128)(2,1)}, bf16[1,64,128,128]{3,2,1,0:T(8,128)(2,1)S(1)}, u32[]{:S(2)}) copy-start(bf16[1,64,128,128]{3,2,1,0:T(8,128)(2,1)S(1)} %get-tuple-element.483) | copy-start | bytes 6291460 | tf_op jit(solution)/shard_map/while
  780.9 14.7 %copy-start.1 = (f32[8192,128]{1,0:T(8,128)}, f32[8192,128]{1,0:T(8,128)S(1)}, u32[]{:S(2)}) copy-start(f32[8192,128]{1,0:T(8,128)S(1)} %get-tuple-element.485) | copy-start | bytes 12582916 | tf_op jit(solution)/shard_map/while
  806.3 22.8 %copy-start.2 = (f32[8192,128]{1,0:T(8,128)S(1)}, f32[8192,128]{1,0:T(8,128)}, u32[]{:S(2)}) copy-start(f32[8192,128]{1,0:T(8,128)} %copy-done.1) | copy-start | bytes 12582916 | tf_op jit(solution)/shard_map/while
  806.3 22.8 %copy-start.10 = (bf16[128,1024]{1,0:T(8,128)(2,1)S(1)}, bf16[128,1024]{1,0:T(8,128)(2,1)}, u32[]{:S(2)}) copy-start(bf16[128,1024]{1,0:T(8,128)(2,1)} %get-tuple-element.557) | copy-start | bytes 786436 | tf_op jit(solution)/shard_map/while
  829.1 13.3 %copy-start.5 = (f32[8192,128]{1,0:T(8,128)S(1)}, f32[8192,128]{1,0:T(8,128)}, u32[]{:S(2)}) copy-start(f32[8192,128]{1,0:T(8,128)} %fusion.124) | copy-start | bytes 12582916 | tf_op jit(solution)/shard_map/while
  861.7 7.8 copy-start.3
  861.7 7.8 copy-start.26
  882.1 6.9 copy-start.27
  889.8 62.7 %copy-start.17 = (bf16[32,384]{1,0:T(8,128)(2,1)S(1)}, bf16[32,384]{1,0:T(8,128)(2,1)}, u32[]{:S(2)}) copy-start(bf16[32,384]{1,0:T(8,128)(2,1)} %param.20) | copy-start | bytes 73732
  889.8 62.7 %copy-start.35 = (f32[32]{0:T(128)S(1)}, f32[32]{0:T(128)}, u32[]{:S(2)}) copy-start(f32[32]{0:T(128)} %copy-done.34) | copy-start | bytes 388
  918.9 218.1 %all-reduce.3.cloned.1.call-start = ((), (), s32[]{:S(2)}) async-start(), calls=%async_computation.5 | async-start | bytes 16646144 | tf_op jit(solution)/shard_map/psum | solution.py:256
  958.0 41.4 %copy-start.12 = (bf16[384,1536]{1,0:T(8,128)(2,1)S(1)}, bf16[384,1536]{1,0:T(8,128)(2,1)}, u32[]{:S(2)}) copy-start(bf16[384,1536]{1,0:T(8,128)(2,1)} %param.29) | copy-start | bytes 3538948
  (45 other events, 117.8 us)
Sparse Core Ops, SparseCore 0:
  919.0 28.1 reduce-scatter.1
  958.1 178.7 all-reduce.2
where the time goes:
time: 1170 us; the launch traced here: 1150 us
  blocking collectives  402 us (34%)
  matrix products  371 us (32%)
  waiting for transfers between devices  162 us (14%)
  local copies, waits for them, and re-layouts  102 us (9%)
  other arithmetic  81.1 us (7%)
  loops' own time  17.3 us (1%)
  between operations  14.7 us (1%)
    dot_general x17, matrix products, product_right(): lax.dot_general(matrix_a, matrix_b, (((1,), (1,)), ((), ())), preferred_e...  162 us
    psum x1, waiting for transfers between devices, local(): lax.psum((up_gate_sum, down_sum, head_sum, rel_sum, prow_sum, pcol_sum),...  136 us
    dot_general x17, matrix products, product_left(): lax.dot_general(matrix_a, matrix_b, (((0,), (0,)), ((), ())), preferred_e...  131 us
    all_to_all x1, blocking collectives, local(): lax.all_to_all(distance_part, 'col', split_axis=0, concat_axis=1, tiled=T...  100 us
    all_to_all x1, blocking collectives, local(): lax.all_to_all(strips, ('row', 'col'), split_axis=1, concat_axis=0, tiled...  98.3 us
    all_gather x1, blocking collectives, local(): row_proj = lax.all_gather(row_piece, 'col', axis=0, tiled=True)  94.8 us
    dot_general x13, matrix products, product(): return jnp.dot(matrix_a, matrix_b, preferred_element_type=jnp.float32)  61.4 us
    all_gather x1, blocking collectives, local(): col_whole = lax.all_gather(col_piece, ('row', 'col'), axis=0, tiled=True)  40 us
  transfers between devices with their start and end apart: 3, of which 2 were waited for; matrix products, arithmetic and copies ran while one was open for 1% of the time, Pallas kernels for 0%

commit v1 on v0

--- a/solution.py
+++ b/solution.py
@@ -183,7 +183,15 @@
     masked = logit_cotangent * pair_mask[:, :, None].astype(jnp.bfloat16)
     distance_part = masked[:, :, bin_count:].reshape(tile_rows, tile_cols * bin_count)
     strips = lax.all_to_all(distance_part, "col", split_axis=0, concat_axis=1, tiled=True)
-    columns = lax.all_to_all(strips, ("row", "col"), split_axis=1, concat_axis=0, tiled=True)
+    columns = jnp.concatenate(
+        lax.all_to_all(
+            jnp.stack(jnp.split(strips, lax.axis_size(("row", "col")), axis=1)),
+            ("row", "col"),
+            0,
+            0,
+        ),
+        axis=0,
+    )
     returned = lax.all_to_all(columns, "col", split_axis=0, concat_axis=1, tiled=True)
     mirrored = returned.reshape(tile_cols, tile_rows, bin_count).transpose(1, 0, 2)
     up_gate = jnp.concatenate([pair_up, pair_gate], axis=1)

time: 1170 us -> 1150 us (0.983)
  local copies, waits for them, and re-layouts: 102 us -> 85.6 us
    all_to_all x2 -> x0, local copies, waits for them, and re-layouts: 12.4 us -> none  [local(): lax.all_to_all(strips, ('row', 'col'), split_axis=1, concat_axis=0, tiled...]
where the time goes in v1:
time: 1150 us; the launch traced here: 1140 us
  blocking collectives  402 us (35%)
  matrix products  371 us (32%)
  waiting for transfers between devices  162 us (14%)
  local copies, waits for them, and re-layouts  85.6 us (7%)
  other arithmetic  81.1 us (7%)
  loops' own time  17.3 us (2%)
  between operations  15 us (1%)
    dot_general x17, matrix products, product_right(): lax.dot_general(matrix_a, matrix_b, (((1,), (1,)), ((), ())), preferred_e...  162 us
    psum x1, waiting for transfers between devices, local(): lax.psum((up_gate_sum, down_sum, head_sum, rel_sum, prow_sum, pcol_sum),...  136 us
    dot_general x17, matrix products, product_left(): lax.dot_general(matrix_a, matrix_b, (((0,), (0,)), ((), ())), preferred_e...  131 us
    all_to_all x1, blocking collectives, local(): lax.all_to_all(distance_part, 'col', split_axis=0, concat_axis=1, tiled=T...  100 us
    all_to_all x1, blocking collectives, local(): lax.all_to_all(jnp.stack(jnp.split(strips, lax.axis_size(('row', 'col')),...  98.3 us
    all_gather x1, blocking collectives, local(): row_proj = lax.all_gather(row_piece, 'col', axis=0, tiled=True)  94.7 us
    dot_general x13, matrix products, product(): return jnp.dot(matrix_a, matrix_b, preferred_element_type=jnp.float32)  61.4 us
    psum x1, blocking collectives, local(): lax.psum((up_gate_sum, down_sum, head_sum, rel_sum, prow_sum, pcol_sum),...  40 us
  transfers between devices with their start and end apart: 3, of which 2 were waited for; matrix products, arithmetic and copies ran while one was open for 1% of the time, Pallas kernels for 0%

profile of v1, /device:TPU:0, one launch (start us, length us, event | category | flops | bytes accessed | tf_op | source)
XLA Modules:
  0.0 1139.0 jit_solution(9900168258754778855)
XLA Ops:
  8.2 8.6 broadcast_multiply_fusion.3
  16.8 9.9 slice.44
  26.8 12.1 %all_to_all.29 = bf16[8,32,8192]{2,1,0:T(8,128)(2,1)} reshape(bf16[256,128,64]{2,1,0:T(8,128)(2,1)} %slice.44) | data formatting | bytes 8388608 | tf_op jit(solution)/shard_map/all_to_all | solution.py:185
  38.8 100.3 %all_to_all.40 = bf16[8,32,8192]{2,1,0:T(8,128)(2,1)S(1)} all-to-all(bf16[8,32,8192]{2,1,0:T(8,128)(2,1)} %all_to_all.29), channel_id=1, replica_groups=mesh['row'=4,'col'=8] {'col'}, dimensions={0} | all-to-all | bytes 8388608 | tf_op jit(solution)/shard_map/all_to_all | solution.py:185
  140.2 98.3 %all_to_all.41 = bf16[32,32,2048]{2,1,0:T(8,128)(2,1)} all-to-all(bf16[32,32,2048]{2,1,0:T(8,128)(2,1)S(1)} %fusion.31), channel_id=1, replica_groups=mesh['row'=4,'col'=8] {'row','col'}, dimensions={0} | all-to-all | bytes 8388608 | tf_op jit(solution)/shard_map/all_to_all | solution.py:187
  238.5 6.5 copy.37
  245.0 4.7 all-to-all-start.2
  256.0 94.7 %all_gather.9 = bf16[256,128]{1,0:T(8,128)(2,1)} all-gather(bf16[32,128]{1,0:T(8,128)(2,1)S(1)} %convolution_convert_fusion.1), channel_id=1, replica_groups=mesh['row'=4,'col'=8] {'col'}, dimensions={0}, use_global_device_ids=true | all-gather | bytes 73728 | tf_op jit(solution)/shard_map/all_gather | solution.py:180
  350.9 40.0 %all_gather.10 = bf16[1024,128]{1,0:T(8,128)(2,1)S(1)} all-gather(bf16[32,128]{1,0:T(8,128)(2,1)S(1)} %convolution_convert_fusion), channel_id=1, replica_groups=mesh['row'=4,'col'=8] {'row','col'}, dimensions={0}, use_global_device_ids=true | all-gather | bytes 270336 | tf_op jit(solution)/shard_map/all_gather | solution.py:181
  391.7 482.4 %while.23 = (s32[]{:T(128)}, f32[128,128]{1,0:T(8,128)}, f32[128,1024]{1,0:T(8,128)}, f32[512,128]{1,0:T(8,128)}, f32[128,128]{1,0:T(8,128)}, /*index=5*/f32[65,...) while((s32[]{:T(128)}, f32[128,128]{1,0:T(8,128)}, ...), condition=%wide.region_8.9_spmd.clone, body=%wide.region_1.8_spmd.clone.sunk | while | flops 11331420160 | bytes 375022848 | solution.py:241
  418.3 12.2 %fusion.159 = f32[8192,1024]{0,1:T(8,128)} fusion(bf16[128,1024]{1,0:T(8,128)(2,1)S(1)} %copy-done.9, f32[8192,128]{1,0:T(8,128)S(1)} %get-tuple-element.454, f32[8192]{0:T(1024)S(1)} %add_rsqrt_fusion.3, f32[8192]{0:T(1024)S(1)} %broadcast_multiply_fusion.13), kind=kOutput, calls=%fused_computation.53.clone.1 | convolution fusion | flops 2150629376 | bytes 38076416 | tf_op jit(solution)/shard_map/while/body/eval_jaxpr/dot_general | solution.py:15
  441.1 22.8 %multiply_convert_fusion.7 = (bf16[8192,512]{0,1:T(8,128)(2,1)}, bf16[8192,512]{0,1:T(8,128)(2,1)}, bf16[8192,512]{0,1:T(8,128)(2,1)}) fusion(f32[8192,1024]{0,1:T(8,128)} %fusion.159, bf16[512,128]{1,0:T(8,128)(2,1)S(1)} %get-tuple-element.525, f32[8192,128]{1,0:T(8,128)} %fusion.156), kind=kOutput, calls=%fused_computation.3.clone.1 | convolution fusion | flops 1137704960 | bytes 63045632 | tf_op jit(solution)/shard_map/while/body/eval_jaxpr/dot_general | solution.py:25
  463.9 13.2 %fusion.160 = (f32[8192]{0:T(1024)S(1)}, f32[8192]{0:T(1024)S(1)}, f32[8192,128]{1,0:T(8,128)S(1)}) fusion(f32[8192]{0:T(1024)S(1)} %add_rsqrt_fusion.3, f32[8192,128]{1,0:T(8,128)S(1)} %copy-done.2, f32[8192]{0:T(1024)S(1)} %broadcast_multiply_fusion.13, bf16[128,1024]{1,0:T(8,128)(2,1)S(1)} %copy-done.10, ...), kind=kOutput, calls=%fused_computation.172.clone.1 | convolution fusion | flops 2186264576 | bytes 25559040 | tf_op jit(solution)/shard_map/while/body/eval_jaxpr/dot_general | solution.py:25
  477.2 5.0 bitcast_reduce_fusion.2
  485.3 11.2 fusion.162
  496.6 7.8 convolution_add_fusion.7
  504.3 12.5 %fusion.161 = f32[128,1024]{1,0:T(8,128)S(1)} fusion(bf16[8192,512]{0,1:T(8,128)(2,1)} %get-tuple-element.456, bf16[8192,512]{0,1:T(8,128)(2,1)} %get-tuple-element.457, f32[128,1024]{1,0:T(8,128)S(1)} %copy-done.26, pred[]{:T(512)S(6)} %compare.3, f32[8192,128]{1,0:T(8,128)S(1)} %copy-done.3, f32[8192]{0:T(1024)S(1)} %add_rsqrt_fusion.3, ...), kind=kOutput, calls=%fused_computation.23.clone.1 | convolution fusion | flops 2184445952 | bytes 22085632 | tf_op jit(solution)/shard_map/while/body/eval_jaxpr/dot_general | solution.py:19
  519.6 4.2 fusion.163
  534.8 12.2 %fusion.159 = f32[8192,1024]{0,1:T(8,128)} fusion(bf16[128,1024]{1,0:T(8,128)(2,1)S(1)} %copy-done.9, f32[8192,128]{1,0:T(8,128)S(1)} %get-tuple-element.454, f32[8192]{0:T(1024)S(1)} %add_rsqrt_fusion.3, f32[8192]{0:T(1024)S(1)} %broadcast_multiply_fusion.13), kind=kOutput, calls=%fused_computation.53.clone.1 | convolution fusion | flops 2150629376 | bytes 38076416 | tf_op jit(solution)/shard_map/while/body/eval_jaxpr/dot_general | solution.py:15
  557.7 22.8 %multiply_convert_fusion.7 = (bf16[8192,512]{0,1:T(8,128)(2,1)}, bf16[8192,512]{0,1:T(8,128)(2,1)}, bf16[8192,512]{0,1:T(8,128)(2,1)}) fusion(f32[8192,1024]{0,1:T(8,128)} %fusion.159, bf16[512,128]{1,0:T(8,128)(2,1)S(1)} %get-tuple-element.525, f32[8192,128]{1,0:T(8,128)} %fusion.156), kind=kOutput, calls=%fused_computation.3.clone.1 | convolution fusion | flops 1137704960 | bytes 63045632 | tf_op jit(solution)/shard_map/while/body/eval_jaxpr/dot_general | solution.py:25
  580.5 13.2 %fusion.160 = (f32[8192]{0:T(1024)S(1)}, f32[8192]{0:T(1024)S(1)}, f32[8192,128]{1,0:T(8,128)S(1)}) fusion(f32[8192]{0:T(1024)S(1)} %add_rsqrt_fusion.3, f32[8192,128]{1,0:T(8,128)S(1)} %copy-done.2, f32[8192]{0:T(1024)S(1)} %broadcast_multiply_fusion.13, bf16[128,1024]{1,0:T(8,128)(2,1)S(1)} %copy-done.10, ...), kind=kOutput, calls=%fused_computation.172.clone.1 | convolution fusion | flops 2186264576 | bytes 25559040 | tf_op jit(solution)/shard_map/while/body/eval_jaxpr/dot_general | solution.py:25
  593.7 5.0 bitcast_reduce_fusion.2
  601.9 11.2 fusion.162
  613.1 7.8 convolution_add_fusion.7
  620.9 12.5 %fusion.161 = f32[128,1024]{1,0:T(8,128)S(1)} fusion(bf16[8192,512]{0,1:T(8,128)(2,1)} %get-tuple-element.456, bf16[8192,512]{0,1:T(8,128)(2,1)} %get-tuple-element.457, f32[128,1024]{1,0:T(8,128)S(1)} %copy-done.26, pred[]{:T(512)S(6)} %compare.3, f32[8192,128]{1,0:T(8,128)S(1)} %copy-done.3, f32[8192]{0:T(1024)S(1)} %add_rsqrt_fusion.3, ...), kind=kOutput, calls=%fused_computation.23.clone.1 | convolution fusion | flops 2184445952 | bytes 22085632 | tf_op jit(solution)/shard_map/while/body/eval_jaxpr/dot_general | solution.py:19
  636.1 4.2 fusion.163
  651.4 12.2 %fusion.159 = f32[8192,1024]{0,1:T(8,128)} fusion(bf16[128,1024]{1,0:T(8,128)(2,1)S(1)} %copy-done.9, f32[8192,128]{1,0:T(8,128)S(1)} %get-tuple-element.454, f32[8192]{0:T(1024)S(1)} %add_rsqrt_fusion.3, f32[8192]{0:T(1024)S(1)} %broadcast_multiply_fusion.13), kind=kOutput, calls=%fused_computation.53.clone.1 | convolution fusion | flops 2150629376 | bytes 38076416 | tf_op jit(solution)/shard_map/while/body/eval_jaxpr/dot_general | solution.py:15
  674.2 22.8 %multiply_convert_fusion.7 = (bf16[8192,512]{0,1:T(8,128)(2,1)}, bf16[8192,512]{0,1:T(8,128)(2,1)}, bf16[8192,512]{0,1:T(8,128)(2,1)}) fusion(f32[8192,1024]{0,1:T(8,128)} %fusion.159, bf16[512,128]{1,0:T(8,128)(2,1)S(1)} %get-tuple-element.525, f32[8192,128]{1,0:T(8,128)} %fusion.156), kind=kOutput, calls=%fused_computation.3.clone.1 | convolution fusion | flops 1137704960 | bytes 63045632 | tf_op jit(solution)/shard_map/while/body/eval_jaxpr/dot_general | solution.py:25
  697.0 13.2 %fusion.160 = (f32[8192]{0:T(1024)S(1)}, f32[8192]{0:T(1024)S(1)}, f32[8192,128]{1,0:T(8,128)S(1)}) fusion(f32[8192]{0:T(1024)S(1)} %add_rsqrt_fusion.3, f32[8192,128]{1,0:T(8,128)S(1)} %copy-done.2, f32[8192]{0:T(1024)S(1)} %broadcast_multiply_fusion.13, bf16[128,1024]{1,0:T(8,128)(2,1)S(1)} %copy-done.10, ...), kind=kOutput, calls=%fused_computation.172.clone.1 | convolution fusion | flops 2186264576 | bytes 25559040 | tf_op jit(solution)/shard_map/while/body/eval_jaxpr/dot_general | solution.py:25
  710.3 5.0 bitcast_reduce_fusion.2
  718.4 11.2 fusion.162
  729.6 7.8 convolution_add_fusion.7
  737.4 12.5 %fusion.161 = f32[128,1024]{1,0:T(8,128)S(1)} fusion(bf16[8192,512]{0,1:T(8,128)(2,1)} %get-tuple-element.456, bf16[8192,512]{0,1:T(8,128)(2,1)} %get-tuple-element.457, f32[128,1024]{1,0:T(8,128)S(1)} %copy-done.26, pred[]{:T(512)S(6)} %compare.3, f32[8192,128]{1,0:T(8,128)S(1)} %copy-done.3, f32[8192]{0:T(1024)S(1)} %add_rsqrt_fusion.3, ...), kind=kOutput, calls=%fused_computation.23.clone.1 | convolution fusion | flops 2184445952 | bytes 22085632 | tf_op jit(solution)/shard_map/while/body/eval_jaxpr/dot_general | solution.py:19
  752.7 4.2 fusion.163
  767.9 12.2 %fusion.159 = f32[8192,1024]{0,1:T(8,128)} fusion(bf16[128,1024]{1,0:T(8,128)(2,1)S(1)} %copy-done.9, f32[8192,128]{1,0:T(8,128)S(1)} %get-tuple-element.454, f32[8192]{0:T(1024)S(1)} %add_rsqrt_fusion.3, f32[8192]{0:T(1024)S(1)} %broadcast_multiply_fusion.13), kind=kOutput, calls=%fused_computation.53.clone.1 | convolution fusion | flops 2150629376 | bytes 38076416 | tf_op jit(solution)/shard_map/while/body/eval_jaxpr/dot_general | solution.py:15
  790.8 22.8 %multiply_convert_fusion.7 = (bf16[8192,512]{0,1:T(8,128)(2,1)}, bf16[8192,512]{0,1:T(8,128)(2,1)}, bf16[8192,512]{0,1:T(8,128)(2,1)}) fusion(f32[8192,1024]{0,1:T(8,128)} %fusion.159, bf16[512,128]{1,0:T(8,128)(2,1)S(1)} %get-tuple-element.525, f32[8192,128]{1,0:T(8,128)} %fusion.156), kind=kOutput, calls=%fused_computation.3.clone.1 | convolution fusion | flops 1137704960 | bytes 63045632 | tf_op jit(solution)/shard_map/while/body/eval_jaxpr/dot_general | solution.py:25
  813.6 13.2 %fusion.160 = (f32[8192]{0:T(1024)S(1)}, f32[8192]{0:T(1024)S(1)}, f32[8192,128]{1,0:T(8,128)S(1)}) fusion(f32[8192]{0:T(1024)S(1)} %add_rsqrt_fusion.3, f32[8192,128]{1,0:T(8,128)S(1)} %copy-done.2, f32[8192]{0:T(1024)S(1)} %broadcast_multiply_fusion.13, bf16[128,1024]{1,0:T(8,128)(2,1)S(1)} %copy-done.10, ...), kind=kOutput, calls=%fused_computation.172.clone.1 | convolution fusion | flops 2186264576 | bytes 25559040 | tf_op jit(solution)/shard_map/while/body/eval_jaxpr/dot_general | solution.py:25
  826.8 5.0 bitcast_reduce_fusion.2
  835.0 11.2 fusion.162
  846.2 7.8 convolution_add_fusion.7
  854.0 12.5 %fusion.161 = f32[128,1024]{1,0:T(8,128)S(1)} fusion(bf16[8192,512]{0,1:T(8,128)(2,1)} %get-tuple-element.456, bf16[8192,512]{0,1:T(8,128)(2,1)} %get-tuple-element.457, f32[128,1024]{1,0:T(8,128)S(1)} %copy-done.26, pred[]{:T(512)S(6)} %compare.3, f32[8192,128]{1,0:T(8,128)S(1)} %copy-done.3, f32[8192]{0:T(1024)S(1)} %add_rsqrt_fusion.3, ...), kind=kOutput, calls=%fused_computation.23.clone.1 | convolution fusion | flops 2184445952 | bytes 22085632 | tf_op jit(solution)/shard_map/while/body/eval_jaxpr/dot_general | solution.py:19
  869.2 4.2 fusion.163
  874.9 14.0 %psum.56 = bf16[128,128]{1,0:T(8,128)(2,1)S(1)} all-reduce(bf16[128,128]{1,0:T(8,128)(2,1)S(1)} %convert_element_type.121), channel_id=1, replica_groups=mesh['row'=4,'col'=8] {'row'}, use_global_device_ids=true, to_apply=%region_10.11 | all-reduce | flops 16384 | bytes 65536 | tf_op jit(solution)/shard_map/psum | solution.py:249
  888.9 14.2 %all_gather.11 = bf16[1024,128]{1,0:T(8,128)(2,1)S(1)} all-gather(bf16[128,128]{1,0:T(8,128)(2,1)S(1)} %psum.56), channel_id=1, replica_groups=mesh['row'=4,'col'=8] {'col'}, dimensions={0}, use_global_device_ids=true | all-gather | bytes 294912 | tf_op jit(solution)/shard_map/all_gather | solution.py:250
  904.8 26.6 %reduce-scatter.2.cloned.1.call-done = bf16[32,128]{1,0:T(8,128)(2,1)} async-done(((bf16[256,128]{1,0:T(8,128)(2,1)}), bf16[32,128]{1,0:T(8,128)(2,1)}) %reduce-scatter.2.cloned.1.call-update) | async-done | bytes 8208 | tf_op jit(solution)/shard_map/reduce_scatter | solution.py:246
  937.9 3.4 pad_maximum_fusion.8
  943.0 40.0 %psum.60 = f32[65,128]{1,0:T(8,128)S(1)} all-reduce(f32[65,128]{1,0:T(8,128)S(1)} %copy-done.20), channel_id=1, replica_groups=mesh['row'=4,'col'=8] {'row','col'}, use_global_device_ids=true, to_apply=%region_15.16 | all-reduce | flops 8320 | bytes 66560 | tf_op jit(solution)/shard_map/psum | solution.py:264
  985.5 135.8 %all-reduce.3.cloned.1.call-done = (f32[128,1024]{1,0:T(8,128)}, f32[512,128]{1,0:T(8,128)}, f32[128,128]{1,0:T(8,128)}, f32[384,128]{1,0:T(8,128)}, f32[384,128]{1,0:T(8,128)}, /*index=5*/f32[3,384,1536]{2,1,0:T(8,128)}) async-done(((f32[128,1024]{1,0:T(8,128)}, f32[512,128]{1,0:T(8,128)}, f32[128,128]{1,0:T(8,128)}, f32[384,128]{1,0:T(8,128)}, f32[384,128]{1,0:T(8,128)}, ...) | async-done | bytes 8323088 | tf_op jit(solution)/shard_map/psum | solution.py:264
  (344 shorter events, 141.7 us)
Async XLA Ops:
  7.2 246.0 %copy-start = (bf16[384,1536]{1,0:T(8,128)(2,1)S(1)}, bf16[384,1536]{1,0:T(8,128)(2,1)}, u32[]{:S(2)}) copy-start(bf16[384,1536]{1,0:T(8,128)(2,1)} %param.30) | copy-start | bytes 3538948
  245.0 7.8 copy-start.16
  245.0 7.9 copy-start.11
  245.0 146.7 %all-to-all-start.2 = ((bf16[8,128,2048]{1,2,0:T(8,128)(2,1)}), bf16[8,128,2048]{1,2,0:T(8,128)(2,1)}, u32[]{:S(2)}, u32[]{:S(2)}) async-start(bf16[8,128,2048]{1,2,0:T(8,128)(2,1)} %copy.37), calls=%async_computation.2 | async-start | bytes 8388608 | tf_op jit(solution)/shard_map/all_to_all | solution.py:195
  249.7 101.1 %copy-start.30 = (bf16[384,128]{1,0:T(8,128)(2,1)S(1)}, bf16[384,128]{1,0:T(8,128)(2,1)}, u32[]{:S(2)}) copy-start(bf16[384,128]{1,0:T(8,128)(2,1)} %param.28) | copy-start | bytes 294916
  249.7 141.2 %copy-start.31 = (bf16[128,512]{1,0:T(8,128)(2,1)S(1)}, bf16[128,512]{1,0:T(8,128)(2,1)}, u32[]{:S(2)}) copy-start(bf16[128,512]{1,0:T(8,128)(2,1)} %param.23) | copy-start | bytes 393220
  249.7 141.2 %copy-start.32 = (bf16[128,512]{1,0:T(8,128)(2,1)S(1)}, bf16[128,512]{1,0:T(8,128)(2,1)}, u32[]{:S(2)}) copy-start(bf16[128,512]{1,0:T(8,128)(2,1)} %param.22) | copy-start | bytes 393220
  249.7 141.9 %copy-start.13 = (bf16[512,128]{1,0:T(8,128)(2,1)S(1)}, bf16[512,128]{1,0:T(8,128)(2,1)}, u32[]{:S(2)}) copy-start(bf16[512,128]{1,0:T(8,128)(2,1)} %param.24) | copy-start | bytes 393220
  249.7 681.7 %reduce-scatter.2.cloned.1.call-start = ((), (), s32[]{:S(2)}) async-start(), calls=%async_computation.4 | async-start | bytes 73728 | tf_op jit(solution)/shard_map/reduce_scatter | solution.py:246
  253.2 138.4 %copy-start.23 = (f32[32,1536]{1,0:T(8,128)}, f32[32,1536]{1,0:T(8,128)S(1)}, u32[]{:S(2)}) copy-start(f32[32,1536]{1,0:T(8,128)S(1)} %fusion.84) | copy-start | bytes 589828
  254.3 137.4 %copy-start.21 = (bf16[32,1536]{1,0:T(8,128)(2,1)}, bf16[32,1536]{1,0:T(8,128)(2,1)S(1)}, u32[]{:S(2)}) copy-start(bf16[32,1536]{1,0:T(8,128)(2,1)S(1)} %get-tuple-element.319) | copy-start | bytes 294916
  255.9 135.8 %copy-start.24 = (bf16[32,384]{1,0:T(8,128)(2,1)}, bf16[32,384]{1,0:T(8,128)(2,1)S(1)}, u32[]{:S(2)}) copy-start(bf16[32,384]{1,0:T(8,128)(2,1)S(1)} %fusion.26) | copy-start | bytes 73732
  410.4 27.5 %copy-start.6 = (bf16[1,64,128,128]{3,2,1,0:T(8,128)(2,1)}, bf16[1,64,128,128]{3,2,1,0:T(8,128)(2,1)S(1)}, u32[]{:S(2)}) copy-start(bf16[1,64,128,128]{3,2,1,0:T(8,128)(2,1)S(1)} %get-tuple-element.452) | copy-start | bytes 6291460 | tf_op jit(solution)/shard_map/while
  415.8 14.7 %copy-start.1 = (f32[8192,128]{1,0:T(8,128)}, f32[8192,128]{1,0:T(8,128)S(1)}, u32[]{:S(2)}) copy-start(f32[8192,128]{1,0:T(8,128)S(1)} %get-tuple-element.454) | copy-start | bytes 12582916 | tf_op jit(solution)/shard_map/while
  441.1 22.8 %copy-start.2 = (f32[8192,128]{1,0:T(8,128)S(1)}, f32[8192,128]{1,0:T(8,128)}, u32[]{:S(2)}) copy-start(f32[8192,128]{1,0:T(8,128)} %copy-done.1) | copy-start | bytes 12582916 | tf_op jit(solution)/shard_map/while
  441.1 22.8 %copy-start.10 = (bf16[128,1024]{1,0:T(8,128)(2,1)S(1)}, bf16[128,1024]{1,0:T(8,128)(2,1)}, u32[]{:S(2)}) copy-start(bf16[128,1024]{1,0:T(8,128)(2,1)} %get-tuple-element.526) | copy-start | bytes 786436 | tf_op jit(solution)/shard_map/while
  463.9 13.3 %copy-start.5 = (f32[8192,128]{1,0:T(8,128)S(1)}, f32[8192,128]{1,0:T(8,128)}, u32[]{:S(2)}) copy-start(f32[8192,128]{1,0:T(8,128)} %fusion.156) | copy-start | bytes 12582916 | tf_op jit(solution)/shard_map/while
  496.6 7.8 copy-start.3
  496.6 7.8 copy-start.26
  516.9 6.9 copy-start.27
  527.0 27.5 %copy-start.6 = (bf16[1,64,128,128]{3,2,1,0:T(8,128)(2,1)}, bf16[1,64,128,128]{3,2,1,0:T(8,128)(2,1)S(1)}, u32[]{:S(2)}) copy-start(bf16[1,64,128,128]{3,2,1,0:T(8,128)(2,1)S(1)} %get-tuple-element.452) | copy-start | bytes 6291460 | tf_op jit(solution)/shard_map/while
  532.3 14.7 %copy-start.1 = (f32[8192,128]{1,0:T(8,128)}, f32[8192,128]{1,0:T(8,128)S(1)}, u32[]{:S(2)}) copy-start(f32[8192,128]{1,0:T(8,128)S(1)} %get-tuple-element.454) | copy-start | bytes 12582916 | tf_op jit(solution)/shard_map/while
  557.7 22.8 %copy-start.2 = (f32[8192,128]{1,0:T(8,128)S(1)}, f32[8192,128]{1,0:T(8,128)}, u32[]{:S(2)}) copy-start(f32[8192,128]{1,0:T(8,128)} %copy-done.1) | copy-start | bytes 12582916 | tf_op jit(solution)/shard_map/while
  557.7 22.8 %copy-start.10 = (bf16[128,1024]{1,0:T(8,128)(2,1)S(1)}, bf16[128,1024]{1,0:T(8,128)(2,1)}, u32[]{:S(2)}) copy-start(bf16[128,1024]{1,0:T(8,128)(2,1)} %get-tuple-element.526) | copy-start | bytes 786436 | tf_op jit(solution)/shard_map/while
  580.5 13.3 %copy-start.5 = (f32[8192,128]{1,0:T(8,128)S(1)}, f32[8192,128]{1,0:T(8,128)}, u32[]{:S(2)}) copy-start(f32[8192,128]{1,0:T(8,128)} %fusion.156) | copy-start | bytes 12582916 | tf_op jit(solution)/shard_map/while
  613.1 7.8 copy-start.3
  613.1 7.8 copy-start.26
  633.4 6.9 copy-start.27
  643.5 27.5 %copy-start.6 = (bf16[1,64,128,128]{3,2,1,0:T(8,128)(2,1)}, bf16[1,64,128,128]{3,2,1,0:T(8,128)(2,1)S(1)}, u32[]{:S(2)}) copy-start(bf16[1,64,128,128]{3,2,1,0:T(8,128)(2,1)S(1)} %get-tuple-element.452) | copy-start | bytes 6291460 | tf_op jit(solution)/shard_map/while
  648.9 14.7 %copy-start.1 = (f32[8192,128]{1,0:T(8,128)}, f32[8192,128]{1,0:T(8,128)S(1)}, u32[]{:S(2)}) copy-start(f32[8192,128]{1,0:T(8,128)S(1)} %get-tuple-element.454) | copy-start | bytes 12582916 | tf_op jit(solution)/shard_map/while
  674.2 22.8 %copy-start.2 = (f32[8192,128]{1,0:T(8,128)S(1)}, f32[8192,128]{1,0:T(8,128)}, u32[]{:S(2)}) copy-start(f32[8192,128]{1,0:T(8,128)} %copy-done.1) | copy-start | bytes 12582916 | tf_op jit(solution)/shard_map/while
  674.2 22.8 %copy-start.10 = (bf16[128,1024]{1,0:T(8,128)(2,1)S(1)}, bf16[128,1024]{1,0:T(8,128)(2,1)}, u32[]{:S(2)}) copy-start(bf16[128,1024]{1,0:T(8,128)(2,1)} %get-tuple-element.526) | copy-start | bytes 786436 | tf_op jit(solution)/shard_map/while
  697.0 13.3 %copy-start.5 = (f32[8192,128]{1,0:T(8,128)S(1)}, f32[8192,128]{1,0:T(8,128)}, u32[]{:S(2)}) copy-start(f32[8192,128]{1,0:T(8,128)} %fusion.156) | copy-start | bytes 12582916 | tf_op jit(solution)/shard_map/while
  729.6 7.8 copy-start.3
  729.6 7.8 copy-start.26
  750.0 6.9 copy-start.27
  760.1 27.5 %copy-start.6 = (bf16[1,64,128,128]{3,2,1,0:T(8,128)(2,1)}, bf16[1,64,128,128]{3,2,1,0:T(8,128)(2,1)S(1)}, u32[]{:S(2)}) copy-start(bf16[1,64,128,128]{3,2,1,0:T(8,128)(2,1)S(1)} %get-tuple-element.452) | copy-start | bytes 6291460 | tf_op jit(solution)/shard_map/while
  765.4 14.7 %copy-start.1 = (f32[8192,128]{1,0:T(8,128)}, f32[8192,128]{1,0:T(8,128)S(1)}, u32[]{:S(2)}) copy-start(f32[8192,128]{1,0:T(8,128)S(1)} %get-tuple-element.454) | copy-start | bytes 12582916 | tf_op jit(solution)/shard_map/while
  790.8 22.8 %copy-start.2 = (f32[8192,128]{1,0:T(8,128)S(1)}, f32[8192,128]{1,0:T(8,128)}, u32[]{:S(2)}) copy-start(f32[8192,128]{1,0:T(8,128)} %copy-done.1) | copy-start | bytes 12582916 | tf_op jit(solution)/shard_map/while
  790.8 22.8 %copy-start.10 = (bf16[128,1024]{1,0:T(8,128)(2,1)S(1)}, bf16[128,1024]{1,0:T(8,128)(2,1)}, u32[]{:S(2)}) copy-start(bf16[128,1024]{1,0:T(8,128)(2,1)} %get-tuple-element.526) | copy-start | bytes 786436 | tf_op jit(solution)/shard_map/while
  813.5 13.3 %copy-start.5 = (f32[8192,128]{1,0:T(8,128)S(1)}, f32[8192,128]{1,0:T(8,128)}, u32[]{:S(2)}) copy-start(f32[8192,128]{1,0:T(8,128)} %fusion.156) | copy-start | bytes 12582916 | tf_op jit(solution)/shard_map/while
  846.2 7.8 copy-start.3
  846.2 7.8 copy-start.26
  866.5 6.9 copy-start.27
  874.1 62.7 %copy-start.17 = (bf16[32,384]{1,0:T(8,128)(2,1)S(1)}, bf16[32,384]{1,0:T(8,128)(2,1)}, u32[]{:S(2)}) copy-start(bf16[32,384]{1,0:T(8,128)(2,1)} %param.20) | copy-start | bytes 73732
  874.1 62.7 %copy-start.35 = (f32[32]{0:T(128)S(1)}, f32[32]{0:T(128)}, u32[]{:S(2)}) copy-start(f32[32]{0:T(128)} %copy-done.34) | copy-start | bytes 388
  903.1 218.1 %all-reduce.3.cloned.1.call-start = ((), (), s32[]{:S(2)}) async-start(), calls=%async_computation.5 | async-start | bytes 16646144 | tf_op jit(solution)/shard_map/psum | solution.py:264
  942.3 41.4 %copy-start.12 = (bf16[384,1536]{1,0:T(8,128)(2,1)S(1)}, bf16[384,1536]{1,0:T(8,128)(2,1)}, u32[]{:S(2)}) copy-start(bf16[384,1536]{1,0:T(8,128)(2,1)} %param.29) | copy-start | bytes 3538948
  (45 other events, 117.8 us)
Sparse Core Ops, SparseCore 0:
  903.2 28.1 reduce-scatter.1
  942.4 178.8 all-reduce.2
